TPU v7x, 1024 devices: a whole 4x8x16 slice. The times are simulated.
1024 devices in a mesh: dp: 64 (over y_hi, z), ctx: 16 (over x, y_lo, core).
Axes of the slice: x: 4, y: 8 (y_hi: 4, y_lo: 2; y = y_hi * 2 + y_lo), z: 16, core: 2. Of those that a mesh axis runs over, the one named last changes fastest.
Arguments:
- queries: bfloat16 [64, 2048, 16, 128], P('dp', 'ctx'), may hold values from -6 to 6
- keys: bfloat16 [64, 2048, 16, 128], P('dp', 'ctx'), may hold values from -6 to 6
- values: bfloat16 [64, 2048, 16, 128], P('dp', 'ctx'), may hold values from -6 to 6
- out_grad: bfloat16 [64, 2048, 16, 128], P('dp', 'ctx'), may hold values from -0.59765625 to 0.59765625
- gate_weight: bfloat16 [16, 128], P(None, 'dp'), may hold values from -0.5 to 0.5
- head_bias: bfloat16 [16], replicated, as said below
Outputs:
- query_grad: bfloat16 [64, 2048, 16, 128], P('dp', 'ctx')
- key_grad: bfloat16 [64, 2048, 16, 128], P('dp', 'ctx')
- gate_grad: float32 [16, 128], P(None, 'dp')
Inputs may be any that keep to these rules, and one draw needn't show every extreme that they name: `head_bias`: each entry lies between -ln(2048) - 1.5 and -3.5.
All inputs are finite; a program needn't handle non-finite values.
Results may differ from a plain program's by a relative error of at most 0.0038.
The roundings to bfloat16 on the way count: a program that leaves them out, or rounds other values in their place, can miss the bound.
Values may be sent and summed in bfloat16 or wider, within the bound.
A program may use at most 128 MiB of HBM per device.

v0:
```python
import jax
import jax.numpy as jnp
from jax import lax
from jax.sharding import PartitionSpec as P


def carried_in(shard, axis, combine, identity, reverse):
    devices, mine = (lax.axis_size(axis), lax.axis_index(axis))
    everything = jax.tree.map(lambda part: lax.all_gather(part, axis), shard)
    start = jax.tree.map(
        lambda part, zero: jnp.broadcast_to(jnp.asarray(zero, part.dtype), part.shape),
        shard,
        identity,
    )

    def hop(k, before):
        at = devices - 1 - k if reverse else k
        reached = at > mine if reverse else at < mine
        new = combine(before, jax.tree.map(lambda part: part[at], everything))
        return jax.tree.map(lambda a, b: jnp.where(reached, a, b), new, before)

    return lax.fori_loop(0, devices, hop, start)


def gate_logit(keys_block, gate_rows, bias_rows):
    return (
        jnp.sum(keys_block.astype(jnp.float32) * gate_rows.astype(jnp.float32)[None], -1)
        + bias_rows.astype(jnp.float32)[None]
    )


def key_state(keys_block, values_block, cumul):
    tail = jnp.exp(cumul[-1][None] - cumul)[:, :, None]
    scaled = (keys_block.astype(jnp.float32) * tail).astype(jnp.bfloat16)
    return (
        jnp.exp(cumul[-1]),
        jnp.einsum("chd,che->hde", scaled, values_block, preferred_element_type=jnp.float32),
    )


def query_state(queries_block, grads_block, cumul):
    head = jnp.exp(cumul)[:, :, None]
    scaled = (queries_block.astype(jnp.float32) * head).astype(jnp.bfloat16)
    return (
        jnp.exp(cumul[-1]),
        jnp.einsum("chd,che->hde", scaled, grads_block, preferred_element_type=jnp.float32),
    )


def block_grads(
    queries_block, keys_block, values_block, grads_block, cumul, incoming, outgoing, scale
):
    count = queries_block.shape[0]
    rows = lax.broadcasted_iota(jnp.int32, (count, count), 0)
    cols = lax.broadcasted_iota(jnp.int32, (count, count), 1)
    causal = rows >= cols
    trans = cumul.T
    gap = trans[:, :, None] - trans[:, None, :]
    decay = jnp.exp(jnp.where(causal[None], gap, -1e30))
    products = jnp.einsum(
        "the,she->hts", grads_block, values_block, preferred_element_type=jnp.float32
    )
    wround = (scale * products * decay).astype(jnp.bfloat16)
    head = jnp.exp(cumul)[:, :, None]
    tail = jnp.exp(cumul[-1][None] - cumul)[:, :, None]
    in_round = incoming.astype(jnp.bfloat16)
    out_round = outgoing.astype(jnp.bfloat16)
    qgrad = jnp.einsum(
        "hts,shd->thd", wround, keys_block, preferred_element_type=jnp.float32
    ) + scale * head * jnp.einsum(
        "the,hde->thd", grads_block, in_round, preferred_element_type=jnp.float32
    )
    kgrad = jnp.einsum(
        "hts,thd->shd", wround, queries_block, preferred_element_type=jnp.float32
    ) + scale * tail * jnp.einsum(
        "she,hde->shd", values_block, out_round, preferred_element_type=jnp.float32
    )
    dgsum = jnp.sum(queries_block.astype(jnp.float32) * qgrad, -1) - jnp.sum(
        keys_block.astype(jnp.float32) * kgrad, -1
    )
    return (qgrad, kgrad, dgsum)


def finish(qgrad, kgrad, dgsum, after, logit, keys_block, gate_rows):
    total = after[None] + jnp.sum(dgsum, 0)[None] - jnp.cumsum(dgsum, 0) + dgsum
    dlogit = -jax.nn.sigmoid(logit) * total
    rounded = lax.optimization_barrier(kgrad.astype(jnp.bfloat16)).astype(jnp.float32)
    key_out = (rounded + dlogit[:, :, None] * gate_rows.astype(jnp.float32)[None]).astype(
        jnp.bfloat16
    )
    weight_term = jnp.sum(dlogit[:, :, None] * keys_block.astype(jnp.float32), 0)
    return (qgrad.astype(jnp.bfloat16), key_out, weight_term)


def combine(earlier, later):
    return (earlier[0] * later[0], later[0][:, None, None] * earlier[1] + later[1])


def add_totals(earlier, later):
    return earlier + later


def per_device(queries, keys, values, out_grad, gate_weight, head_bias):
    gate_full = lax.all_gather(gate_weight, "dp", axis=1, tiled=True)
    heads, width = (queries.shape[2], queries.shape[3])
    qx, kx, vx, gx = (queries[0], keys[0], values[0], out_grad[0])
    scale = 1.0 / width
    logit = gate_logit(kx, gate_full, head_bias)
    cumul = jnp.cumsum(-jax.nn.softplus(logit), axis=0)
    factor, key_update = key_state(kx, vx, cumul)
    _, query_update = query_state(qx, gx, cumul)
    ones = jnp.ones((heads,), jnp.float32)
    zeros = jnp.zeros((heads, width, width), jnp.float32)
    incoming = carried_in((factor, key_update), "ctx", combine, (ones, zeros), False)[1]
    outgoing = carried_in((factor, query_update), "ctx", combine, (ones, zeros), True)[1]
    qgrad, kgrad, dgsum = block_grads(qx, kx, vx, gx, cumul, incoming, outgoing, scale)
    after = carried_in(jnp.sum(dgsum, 0), "ctx", add_totals, jnp.zeros((heads,), jnp.float32), True)
    qout, kout, term = finish(qgrad, kgrad, dgsum, after, logit, kx, gate_full)
    query_grad, key_grad = (qout[None], kout[None])
    summed = lax.psum(term, ("dp", "ctx"))
    piece = gate_weight.shape[1]
    gate_grad = lax.dynamic_slice_in_dim(summed, lax.axis_index("dp") * piece, piece, 1)
    return (query_grad, key_grad, gate_grad)


def solution(mesh):
    return jax.shard_map(
        per_device,
        mesh=mesh,
        in_specs=(
            P("dp", "ctx", None, None),
            P("dp", "ctx", None, None),
            P("dp", "ctx", None, None),
            P("dp", "ctx", None, None),
            P(None, "dp"),
            P(),
        ),
        out_specs=(P("dp", "ctx", None, None), P("dp", "ctx", None, None), P(None, "dp")),
        check_vma=False,
    )
```

profile of v0, /device:TPU:1, one launch (start us, length us, event | category | flops | bytes accessed | tf_op | source)
XLA Modules:
  0.0 568.6 jit_solution(3678961394848161666)
XLA Ops:
  7.2 1.5 copy.29
  8.7 142.8 %all-gather.3 = bf16[64,2,16]{2,1,0:T(2,128)(2,1)S(1)} all-gather(bf16[1,2,16]{2,1,0:T(2,128)(2,1)} %bitcast.98), channel_id=1, replica_groups=mesh['dp'=64,'ctx'=16] {'dp'}, dimensions={0}, use_global_device_ids=true | all-gather | bytes 4160 | tf_op jit(solution)/shard_map/all_gather | solution.py:104
  153.1 1.3 fusion.15
  154.5 1.5 copy.38
  156.0 2.5 fusion.17
  160.7 47.8 %all-gather.4 = f32[16,1,16]{2,1,0:T(1,128)S(1)} all-gather(f32[1,1,16]{2,1,0:T(1,128)S(1)} %get-tuple-element.440), channel_id=1, replica_groups=mesh['dp'=64,'ctx'=16] {'ctx'}, dimensions={0}, use_global_device_ids=true | all-gather | bytes 1088 | tf_op jit(solution)/shard_map/all_gather | solution.py:9
  208.6 1.7 fusion.7
  211.1 1.5 convolution_bitcast_fusion.3
  212.5 59.9 %all-gather.8.cloned.1.call-done = f32[256,128,128]{2,1,0:T(8,128)} async-done(((f32[16,128,128]{2,1,0:T(8,128)}), f32[256,128,128]{2,1,0:T(8,128)}) %all-gather.8.cloned.1.call-update) | async-done | bytes 16777232 | tf_op jit(solution)/shard_map/all_gather | solution.py:9
  272.5 24.1 %while.46 = (s32[]{:T(128)}, f32[16,128,128]{2,1,0:T(8,128)S(1)}, s32[]{:T(128)}, f32[16,16]{1,0:T(8,128)S(1)}, f32[16,16,128,128]{3,2,1,0:T(8,128)}, /*index=5*/s32[]{:T(128)}, s32[]{:T(128)}) while((s32[]{:T(128)}, f32[16,128,128]{2,1,0:T(8,128)S(1)}, s32[]{:T(128)}, f32[16,16]{1,0:T(8,128)S(1)}, f32[16,16,128,128]{3,2,1,0:T(8,128)}, ...), condition=%wide.region_3.4_spmd.clone, body=%wide.region_2.3_spmd.clone.sunk | while | flops 1048580 | bytes 3146025 | solution.py:22
  272.5 1.5 fusion.44
  274.0 1.5 fusion.44
  275.5 1.5 fusion.44
  277.0 1.5 fusion.44
  278.5 1.5 fusion.44
  280.0 1.5 fusion.44
  281.5 1.5 fusion.44
  283.0 1.5 fusion.44
  284.5 1.5 fusion.44
  286.0 1.5 fusion.44
  287.5 1.5 fusion.44
  289.0 1.5 fusion.44
  290.5 1.5 fusion.44
  292.0 1.5 fusion.44
  293.5 1.5 fusion.44
  295.0 1.6 fusion.44
  296.6 2.9 fusion.9
  299.6 78.8 %all-gather.10.cloned.1.call-done = f32[256,128,128]{2,1,0:T(8,128)} async-done(((f32[16,128,128]{2,1,0:T(8,128)}), f32[256,128,128]{2,1,0:T(8,128)}) %all-gather.10.cloned.1.call-update) | async-done | bytes 16777232 | tf_op jit(solution)/shard_map/all_gather | solution.py:9
  378.4 24.2 %while.47 = (s32[]{:T(128)}, f32[16,128,128]{2,1,0:T(8,128)S(1)}, s32[]{:T(128)}, f32[16,16]{1,0:T(8,128)S(1)}, f32[16,16,128,128]{3,2,1,0:T(8,128)}, /*index=5*/s32[]{:T(128)}, s32[]{:T(128)}, s32[]{:T(128)}, s32[]{:T(128)}) while((s32[]{:T(128)}, f32[16,128,128]{2,1,0:T(8,128)S(1)}, s32[]{:T(128)}, f32[16,16]{1,0:T(8,128)S(1)}, ...), condition=%wide.region_5.6_spmd.clone, body=%wide.region_4.5_spmd.clone.sunk | while | flops 1048584 | bytes 3146087 | solution.py:22
  378.4 1.5 fusion.45
  379.9 1.5 fusion.45
  381.4 1.5 fusion.45
  382.9 1.5 fusion.45
  384.5 1.5 fusion.45
  386.0 1.5 fusion.45
  387.5 1.5 fusion.45
  389.0 1.5 fusion.45
  390.5 1.5 fusion.45
  392.0 1.5 fusion.45
  393.5 1.5 fusion.45
  395.0 1.5 fusion.45
  396.6 1.5 fusion.45
  398.1 1.5 fusion.45
  399.6 1.5 fusion.45
  401.1 1.5 fusion.45
  403.1 1.4 fusion.12
  404.8 26.7 %all-reduce = f32[256]{0:T(256)S(1)} all-reduce(f32[256]{0:T(256)S(1)} %dynamic-update-slice), channel_id=4, replica_groups=mesh['dp'=64,'ctx'=16] {'ctx'}, use_global_device_ids=true, to_apply=%add | all-reduce | flops 256 | bytes 2048
  434.5 125.3 %psum.7 = f32[16,128]{1,0:T(8,128)S(1)} all-reduce(f32[16,128]{1,0:T(8,128)S(1)} %get-tuple-element.441), channel_id=1, replica_groups=mesh['dp'=64,'ctx'=16] {'dp','ctx'}, use_global_device_ids=true, to_apply=%region_13.14 | all-reduce | flops 2048 | bytes 16384 | tf_op jit(solution)/shard_map/psum | solution.py:120
  (97 shorter events, 10.3 us)
Async XLA Ops:
  7.2 145.9 %copy-start = (bf16[1,128,16,128]{3,2,1,0:T(8,128)(2,1)S(1)}, bf16[1,128,16,128]{3,2,1,0:T(8,128)(2,1)}, u32[]{:S(2)}) copy-start(bf16[1,128,16,128]{3,2,1,0:T(8,128)(2,1)} %param.14) | copy-start | bytes 1572868
  7.2 265.3 %all-gather.8.cloned.1.call-start = ((), (), s32[]{:S(2)}) async-start(), calls=%async_computation | async-start | bytes 17825792 | tf_op jit(solution)/shard_map/all_gather | solution.py:9
  154.5 223.9 %all-gather.10.cloned.1.call-start = ((), (), s32[]{:S(2)}) async-start(), calls=%async_computation.1 | async-start | bytes 17825792 | tf_op jit(solution)/shard_map/all_gather | solution.py:9
  156.0 2.6 copy-start.1
  210.3 0.8 copy-start.4
  299.5 103.6 %copy-start.2 = (bf16[1,128,16,128]{1,3,2,0:T(8,128)(2,1)S(1)}, bf16[1,128,16,128]{1,3,2,0:T(8,128)(2,1)}, u32[]{:S(2)}) copy-start(bf16[1,128,16,128]{1,3,2,0:T(8,128)(2,1)} %copy-done.1) | copy-start | bytes 1572868
  299.5 261.1 %copy-start.3 = (bf16[1,128,16,128]{1,3,2,0:T(8,128)(2,1)S(1)}, bf16[1,128,16,128]{1,3,2,0:T(8,128)(2,1)}, u32[]{:S(2)}) copy-start(bf16[1,128,16,128]{1,3,2,0:T(8,128)(2,1)} %get-tuple-element.434) | copy-start | bytes 1572868
Sparse Core Ops, SparseCore 0:
  154.6 117.8 all-gather.7
  275.2 103.1 all-gather.9
where the time goes:
time: 570 us; the launch traced here: 569 us
  blocking collectives  343 us (60%)
  waiting for transfers between devices  139 us (24%)
  other arithmetic  49.3 us (9%)
  between operations  14.9 us (3%)
  matrix products  11.7 us (2%)
  local copies, waits for them, and re-layouts  9.5 us (2%)
    all_gather x1, blocking collectives, per_device(): gate_full = lax.all_gather(gate_weight, 'dp', axis=1, tiled=True)  143 us
    all_gather x2, waiting for transfers between devices, carried_in(): everything = jax.tree.map(lambda part: lax.all_gather(part, axis), shard)  139 us
    psum x1, blocking collectives, per_device(): summed = lax.psum(term, ('dp', 'ctx'))  125 us
    all_gather x1, blocking collectives, carried_in(): everything = jax.tree.map(lambda part: lax.all_gather(part, axis), shard)  47.8 us
    select_n x48, other arithmetic, hop(): return jax.tree.map(lambda a, b: jnp.where(reached, a, b), new, before)  47.1 us
    unnamed x1, blocking collectives  26.7 us
  transfers between devices with their start and end apart: 2, of which 2 were waited for; matrix products, arithmetic and copies ran while one was open for 6% of the time, Pallas kernels for 0%

commit v1 on v0

v1 whole, which is shorter than its diff:
```python
import functools

import jax
import jax.numpy as jnp
from jax import lax
from jax.experimental import pallas as pl
from jax.experimental.pallas import tpu as pltpu
from jax.sharding import PartitionSpec as P

F32 = jnp.float32
BF16 = jnp.bfloat16
MESH = pl.DeviceIdType.MESH
K, V, G, Q = 0, 1, 2, 3
ZN = 16


def iota(shape, dim):
    return lax.broadcasted_iota(jnp.int32, shape, dim)


def dot(a, b, dims, precision=None):
    return lax.dot_general(
        a, b, (dims, ((), ())), precision=precision, preferred_element_type=F32
    )


NN = ((1,), (0,))
NT = ((1,), (1,))
TN = ((0,), (0,))
EXACT = lax.Precision.HIGHEST


def log1p(y):
    u = 1.0 + y
    d = u - 1.0
    return jnp.where(d == 0.0, y, jnp.log(u) * (y / jnp.where(d == 0.0, 1.0, d)))


class Exchange:
    def __init__(self, n, me, where, own, slots, ssem, rsem):
        self.n, self.me, self.where = n, me, where
        self.own, self.slots, self.ssem, self.rsem = own, slots, ssem, rsem

    def copy(self, j, slot, target):
        return pltpu.make_async_remote_copy(
            src_ref=self.own,
            dst_ref=self.slots.at[slot],
            send_sem=self.ssem.at[j],
            recv_sem=self.rsem.at[slot],
            device_id=self.where(target),
            device_id_type=MESH,
        )

    def start(self, row):
        self.own[...] = row
        self.slots[self.me] = row

        def go(j, _):
            self.copy(j, self.me, lax.rem(self.me + j, self.n)).start()
            return 0

        lax.fori_loop(1, self.n, go, 0)

    def finish(self):
        def go(j, _):
            s = lax.rem(self.me + j, self.n)
            self.copy(j, s, s).wait()
            return 0

        lax.fori_loop(1, self.n, go, 0)


def kernel(
    k_in, v_in, g_in, q_in, gw_ref, hb_ref,
    qo_out, ko_out, gg_ref,
    raw, raw32, sb, rb, colb, rowb, lastb, kvr, wts, qf, out_s, out_r, packed, lrow, square,
    wy_own, wy_slots, wz_own, wz_slots, dz_own, dz_slots, dy_own, dy_slots, dc_own, dc_slots,
    lsem, osem, in_s, in_rs, back_s, back_rs, own_sem, own_back,
    wy_s, wy_r, wz_s, wz_r, dz_s, dz_r, dy_s, dy_r, dc_s, dc_r,
):
    yn = wy_slots.shape[0]
    heads = sb.shape[1]
    tok = sb.shape[2]
    width = sb.shape[3]
    scale = 1.0 / width
    i = lax.axis_index("dp")
    c = lax.axis_index("ctx")
    yh = i // ZN
    z = lax.rem(i, ZN)

    def at_ctx(t):
        return {"ctx": t}

    def at_z(t):
        return {"dp": yh * ZN + t}

    def at_y(t):
        return {"dp": t * ZN + z}

    loads = [
        pltpu.make_async_copy(src, raw.at[a], lsem.at[a])
        for a, src in enumerate((k_in, v_in, g_in, q_in))
    ]
    for load in loads:
        load.start()

    barrier = pltpu.get_barrier_semaphore()
    for n, me, where in ((ZN, z, at_z), (yn, yh, at_y), (heads, c, at_ctx)):

        def greet(j, _, n=n, me=me, where=where):
            pl.semaphore_signal(
                barrier, inc=1, device_id=where(lax.rem(me + j, n)), device_id_type=MESH
            )
            return 0

        lax.fori_loop(1, n, greet, 0)

    gw = gw_ref[...].astype(F32)
    picked = jnp.sum(jnp.where(iota(gw.shape, 0) == c, gw, 0.0), axis=0, keepdims=True)
    lane = iota((1, width), 1)
    own_row = jnp.where(lane == 2 * i, picked[:, 0:1], 0.0) + jnp.where(
        lane == 2 * i + 1, picked[:, 1:2], 0.0
    )
    hb = hb_ref[...].astype(F32)
    bias = jnp.sum(jnp.where(iota(hb.shape, 1) == c, hb, 0.0), axis=1, keepdims=True)

    def split_heads(a):
        loads[a].wait()
        raw32[...] = raw[a].astype(F32)
        for h in range(heads):
            sb[a, h] = raw32[pl.ds(h, tok, stride=heads), :].astype(BF16)

    def bulk(a, j, slot, target):
        return pltpu.make_async_remote_copy(
            src_ref=sb.at[a, target],
            dst_ref=rb.at[a, slot],
            send_sem=in_s.at[a, j],
            recv_sem=in_rs.at[a, slot],
            device_id=at_ctx(target),
            device_id_type=MESH,
        )

    def own_in(a):
        return pltpu.make_async_copy(sb.at[a, c], rb.at[a, c], own_sem.at[a])

    def send_heads(a):
        def go(j, _):
            bulk(a, j, c, lax.rem(c + j, heads)).start()
            return 0

        lax.fori_loop(1, heads, go, 0)
        own_in(a).start()

    def wait_heads(a):
        def go(j, _):
            s = lax.rem(c + j, heads)
            bulk(a, j, s, s).wait_recv()
            return 0

        lax.fori_loop(1, heads, go, 0)
        own_in(a).wait()

    wy = Exchange(yn, yh, at_y, wy_own, wy_slots, wy_s, wy_r)
    wz = Exchange(ZN, z, at_z, wz_own, wz_slots, wz_s, wz_r)
    split_heads(K)
    pl.semaphore_wait(barrier, (ZN - 1) + (yn - 1) + (heads - 1))
    wy.start(own_row)
    send_heads(K)
    split_heads(V)
    send_heads(V)
    wy.finish()
    wz.start(jnp.sum(wy_slots[...], axis=0))
    split_heads(G)
    send_heads(G)
    split_heads(Q)
    send_heads(Q)
    wz.finish()
    gate = jnp.sum(wz_slots[...], axis=0)

    wait_heads(K)
    gate8 = jnp.broadcast_to(gate, (8, width)).astype(BF16)
    for b in range(heads):
        lrow[b : b + 1, :] = dot(gate8, rb[K, b], NT)[0:1]
    logit = lrow[...] + bias
    decay = -(jnp.maximum(logit, 0.0) + log1p(jnp.exp(-jnp.abs(logit))))
    upper = (iota((tok, tok), 0) <= iota((tok, tok), 1)).astype(F32)
    cumul = dot(decay, upper, NN, EXACT)
    square[...] = jnp.zeros_like(square)
    square[0:heads, :] = cumul
    cumul_t = square[...].T
    square[0:heads, :] = logit
    logit_t = square[...].T
    for b in range(heads):
        colb[b] = jnp.broadcast_to(cumul_t[:, b : b + 1], (tok, width))
        rowb[b] = cumul[b : b + 1, :]
        lastb[b] = jnp.broadcast_to(cumul[b : b + 1, tok - 1 : tok], (1, width))

    wait_heads(V)

    def forward(b, state):
        kvr[b] = state.astype(BF16)
        tail = jnp.exp(lastb[b] - colb[b])
        scaled = (rb[K, b].astype(F32) * tail).astype(BF16)
        return jnp.exp(lastb[b]) * state + dot(rb[V, b], scaled, TN)

    lax.fori_loop(0, heads, forward, jnp.zeros((width, width), F32), unroll=4)

    wait_heads(G)

    def back(which, j, slot, target):
        return pltpu.make_async_remote_copy(
            src_ref=out_s.at[which, target],
            dst_ref=out_r.at[which, slot],
            send_sem=back_s.at[which, j],
            recv_sem=back_rs.at[which, slot],
            device_id=at_ctx(target),
            device_id_type=MESH,
        )

    def own_out(which):
        return pltpu.make_async_copy(out_s.at[which, c], out_r.at[which, c], own_back.at[which])

    causal = iota((tok, tok), 0) >= iota((tok, tok), 1)

    def query_block(b):
        kx, vx, gx = rb[K, b], rb[V, b], rb[G, b]
        gap = colb[b] - rowb[b]
        fade = jnp.exp(jnp.where(causal, gap, -1e30))
        weight = (scale * dot(gx, vx, NT) * fade).astype(BF16)
        wts[b] = weight
        full = dot(weight, kx, NN) + scale * jnp.exp(colb[b]) * dot(gx, kvr[b], NN)
        qf[b] = full
        out_s[0, b] = full.astype(BF16)

    query_block(c)
    own_out(0).start()

    def query_step(j, _):
        b = lax.rem(c + j, heads)
        query_block(b)
        back(0, j, c, b).start()
        return 0

    lax.fori_loop(1, heads, query_step, 0, unroll=3)

    wait_heads(Q)

    def backward(j, carry):
        b = heads - 1 - j
        state, dg_t = carry
        kx, vx, gx, qx = rb[K, b], rb[V, b], rb[G, b], rb[Q, b]
        col, last = colb[b], lastb[b]
        tail = jnp.exp(last - col)
        kattn = dot(wts[b], qx, TN) + scale * tail * dot(vx, state.astype(BF16), NN)
        out_s[1, b] = kattn.astype(BF16)
        qx32 = qx.astype(F32)
        diff = jnp.sum(qx32 * qf[b] - kx.astype(F32) * kattn, axis=1, keepdims=True)
        dg_t = jnp.where(iota(dg_t.shape, 1) == b, diff, dg_t)
        scaled = (qx32 * jnp.exp(col)).astype(BF16)
        return jnp.exp(last) * state + dot(gx, scaled, TN), dg_t

    zeros = jnp.zeros((width, width), F32)
    _, dg_t = lax.fori_loop(0, heads, backward, (zeros, zeros), unroll=4)

    later = (iota((tok, tok), 0) <= iota((tok, tok), 1)).astype(F32)
    within = dot(later, dg_t, NN, EXACT)
    after_mat = (iota((width, width), 0) > iota((width, width), 1)).astype(F32)
    after = dot(jnp.broadcast_to(within[0:1, :], (8, width)), after_mat, NN, EXACT)
    dlogit = -(within + after[0:1, :]) / (1.0 + jnp.exp(-logit_t))

    total = zeros
    for b in range(heads):
        dcol = jnp.broadcast_to(dlogit[:, b : b + 1], (tok, width))
        total = total + dcol * rb[K, b].astype(F32)
        out_s[1, b] = (out_s[1, b].astype(F32) + dcol * gate).astype(BF16)

    dz = Exchange(ZN, z, at_z, dz_own, dz_slots, dz_s, dz_r)
    dy = Exchange(yn, yh, at_y, dy_own, dy_slots, dy_s, dy_r)
    dc = Exchange(heads, c, at_ctx, dc_own, dc_slots, dc_s, dc_r)
    dz.start(jnp.sum(total, axis=0, keepdims=True))

    def send_key(j, _):
        back(1, j, c, lax.rem(c + j, heads)).start()
        return 0

    lax.fori_loop(1, heads, send_key, 0)
    own_out(1).start()

    outs = (qo_out, ko_out)

    def join_heads(which):
        def go(j, _):
            s = lax.rem(c + j, heads)
            back(which, j, s, s).wait_recv()
            return 0

        lax.fori_loop(1, heads, go, 0)
        own_out(which).wait()
        for h in range(heads):
            raw32[pl.ds(h, tok, stride=heads), :] = out_r[which, h].astype(F32)
        packed[which] = raw32[...].astype(BF16)
        pltpu.make_async_copy(packed.at[which], outs[which], osem.at[which]).start()

    join_heads(0)
    dz.finish()
    dy.start(jnp.sum(dz_slots[...], axis=0))
    dy.finish()
    dc.start(jnp.sum(dy_slots[...], axis=0))
    join_heads(1)
    dc.finish()
    rows = dc_slots[...].reshape(heads, width)
    at = iota((heads, width), 1)
    left = jnp.sum(jnp.where(at == 2 * i, rows, 0.0), axis=1, keepdims=True)
    right = jnp.sum(jnp.where(at == 2 * i + 1, rows, 0.0), axis=1, keepdims=True)
    gg_ref[...] = jnp.where(iota((heads, 2), 1) == 0, left, right)

    def drain(j, _):
        t = lax.rem(c + j, heads)
        for a in range(4):
            bulk(a, j, c, t).wait_send()
        for which in range(2):
            back(which, j, c, t).wait_send()
        return 0

    lax.fori_loop(1, heads, drain, 0)
    for which in range(2):
        pltpu.make_async_copy(packed.at[which], outs[which], osem.at[which]).wait()


def per_device(queries, keys, values, out_grad, gate_weight, head_bias):
    _, tok, heads, width = queries.shape
    yn = lax.axis_size("dp") // ZN
    rows = tok * heads
    flat = [x.reshape(rows, width) for x in (keys, values, out_grad, queries)]
    vm = pltpu.VMEM
    dma = pltpu.SemaphoreType.DMA

    def slots(n):
        return [vm((1, width), F32), vm((n, 1, width), F32)]

    anywhere = pl.BlockSpec(memory_space=pl.ANY)
    inside = pl.BlockSpec(memory_space=pltpu.VMEM)
    qo, ko, gg = pl.pallas_call(
        kernel,
        name="history_grads",
        out_shape=(
            jax.ShapeDtypeStruct((rows, width), BF16),
            jax.ShapeDtypeStruct((rows, width), BF16),
            jax.ShapeDtypeStruct((heads, 2), F32),
        ),
        in_specs=[anywhere] * 4 + [inside] * 2,
        out_specs=(anywhere, anywhere, inside),
        scratch_shapes=[
            vm((4, rows, width), BF16),
            vm((rows, width), F32),
            vm((4, heads, tok, width), BF16),
            vm((4, heads, tok, width), BF16),
            vm((heads, tok, width), F32),
            vm((heads, 1, width), F32),
            vm((heads, 1, width), F32),
            vm((heads, width, width), BF16),
            vm((heads, tok, tok), BF16),
            vm((heads, tok, width), F32),
            vm((2, heads, tok, width), BF16),
            vm((2, heads, tok, width), BF16),
            vm((2, rows, width), BF16),
            vm((heads, width), F32),
            vm((width, width), F32),
            *slots(yn), *slots(ZN), *slots(ZN), *slots(yn), *slots(heads),
            dma((4,)), dma((2,)),
            dma((4, heads)), dma((4, heads)),
            dma((2, heads)), dma((2, heads)),
            dma((4,)), dma((2,)),
            dma((yn,)), dma((yn,)), dma((ZN,)), dma((ZN,)),
            dma((ZN,)), dma((ZN,)), dma((yn,)), dma((yn,)), dma((heads,)), dma((heads,)),
        ],
        compiler_params=pltpu.CompilerParams(
            collective_id=0, has_side_effects=True, vmem_limit_bytes=48 * 1024 * 1024
        ),
    )(*flat, gate_weight, head_bias.reshape(1, heads))
    shape = (1, tok, heads, width)
    return qo.reshape(shape), ko.reshape(shape), gg


def solution(mesh):
    return jax.shard_map(
        per_device,
        mesh=mesh,
        in_specs=(
            P("dp", "ctx", None, None),
            P("dp", "ctx", None, None),
            P("dp", "ctx", None, None),
            P("dp", "ctx", None, None),
            P(None, "dp"),
            P(),
        ),
        out_specs=(P("dp", "ctx", None, None), P("dp", "ctx", None, None), P(None, "dp")),
        check_vma=False,
    )
```

time: 570 us -> 80.9 us (0.14)
  blocking collectives: 343 us -> 0 us
  waiting for transfers between devices: 139 us -> 0 us
  Pallas kernels: 0 us -> 72.2 us
  other arithmetic: 49.3 us -> 0 us
  between operations: 14.9 us -> 0.65 us
  matrix products: 11.7 us -> 0 us
    all_gather x2 -> x0, blocking collectives: 191 us -> none  [the longest x1 143 us: per_device(): gate_full = lax.all_gather(gate_weight, 'dp', axis=1, tiled=True)]
    all_gather x2 -> x0, waiting for transfers between devices: 139 us -> none  [carried_in(): everything = jax.tree.map(lambda part: lax.all_gather(part, axis), shard)]
    psum x1 -> x0, blocking collectives: 125 us -> none  [per_device(): summed = lax.psum(term, ('dp', 'ctx'))]
    pallas_call x0 -> x1, Pallas kernels: none -> 72.2 us  [per_device(): pl.pallas_call(kernel, name='history_grads', out_shape=(jax.ShapeDtypeStr...]
    select_n x48 -> x0, other arithmetic: 47.1 us -> none  [hop(): return jax.tree.map(lambda a, b: jnp.where(reached, a, b), new, before)]
    unnamed x1 -> x0, blocking collectives: 26.7 us -> none
    dot_general x7 -> x0, matrix products: 11.7 us -> none  [the longest x1 2.87 us: block_grads(): jnp.einsum('the,hde->thd', grads_block, in_round, preferred_element_type=...]
  transfers between devices with their start and end apart: 2 -> 0, of which waited for: 2 -> 0; matrix products, arithmetic and copies ran while one was open for 6% -> 0% of each run, Pallas kernels for 0% -> 0%
where the time goes in v1:
time: 80.9 us; the launch traced here: 80.5 us
  Pallas kernels  72.2 us (89%)
  local copies, waits for them, and re-layouts  7.69 us (10%)
    pallas_call x1, Pallas kernels, per_device(): pl.pallas_call(kernel, name='history_grads', out_shape=(jax.ShapeDtypeStr...  72.2 us
    unnamed x16, local copies, waits for them, and re-layouts  7.69 us

profile of v1, /device:TPU:1, one launch (start us, length us, event | category | flops | bytes accessed | tf_op | source)
XLA Modules:
  0.0 80.5 jit_solution(8354617401037094003)
XLA Ops:
  0.6 0.0 copy-start.5
  0.6 0.6 copy-done.5
  1.3 0.0 copy-start.4
  1.3 0.1 copy.9.gw_ref
  1.4 0.6 copy-done.4
  1.9 0.0 copy-start
  1.9 1.0 %copy-done = bf16[1,128,16,128]{3,2,1,0:T(8,128)(2,1)S(1)} copy-done((bf16[1,128,16,128]{3,2,1,0:T(8,128)(2,1)S(1)}, bf16[1,128,16,128]{3,2,1,0:T(8,128)(2,1)}, u32[]{:S(2)}) %copy-start) | copy-done | bytes 524312
  3.0 0.0 copy-start.1
  3.0 1.0 %copy-done.1 = bf16[1,128,16,128]{3,2,1,0:T(8,128)(2,1)S(1)} copy-done((bf16[1,128,16,128]{3,2,1,0:T(8,128)(2,1)S(1)}, bf16[1,128,16,128]{3,2,1,0:T(8,128)(2,1)}, u32[]{:S(2)}) %copy-start.1) | copy-done | bytes 524312
  4.0 0.0 copy-start.2
  4.0 1.0 %copy-done.2 = bf16[1,128,16,128]{3,2,1,0:T(8,128)(2,1)S(1)} copy-done((bf16[1,128,16,128]{3,2,1,0:T(8,128)(2,1)S(1)}, bf16[1,128,16,128]{3,2,1,0:T(8,128)(2,1)}, u32[]{:S(2)}) %copy-start.2) | copy-done | bytes 524312
  5.1 0.0 copy-start.3
  5.1 1.0 %copy-done.3 = bf16[1,128,16,128]{3,2,1,0:T(8,128)(2,1)S(1)} copy-done((bf16[1,128,16,128]{3,2,1,0:T(8,128)(2,1)S(1)}, bf16[1,128,16,128]{3,2,1,0:T(8,128)(2,1)}, u32[]{:S(2)}) %copy-start.3) | copy-done | bytes 524312
  6.1 72.2 %history_grads.1 = (bf16[2048,128]{1,0:T(8,128)(2,1)S(1)}, bf16[2048,128]{1,0:T(8,128)(2,1)S(1)}, f32[16,2]{1,0:T(8,128)S(1)}) custom-call(bf16[2048,128]{1,0:T(8,128)(2,1)S(1)} %bitcast.7, bf16[2048,128]{1,0:T(8,128)(2,1)S(1)} %bitcast.8, bf16[2048,128]{1,0:T(8,128)(2,1)S(1)} %bitcast.9, bf16[2048,128]{1,0:T(8,128)(2,1)S(1)} %bitcast.10, ...), custom_call_target="tpu_custom_call" | custom-call | tf_op jit(solution)/shard_map/history_grads/pallas_call | solution.py:343
  78.3 0.6 copy.10
  78.9 0.8 copy.13
  79.7 0.8 copy.14
Async XLA Ops:
  0.6 0.7 copy-start.5
  1.3 0.7 copy-start.4
  1.9 1.0 %copy-start = (bf16[1,128,16,128]{3,2,1,0:T(8,128)(2,1)S(1)}, bf16[1,128,16,128]{3,2,1,0:T(8,128)(2,1)}, u32[]{:S(2)}) copy-start(bf16[1,128,16,128]{3,2,1,0:T(8,128)(2,1)} %param.7) | copy-start | bytes 1572868
  3.0 1.0 %copy-start.1 = (bf16[1,128,16,128]{3,2,1,0:T(8,128)(2,1)S(1)}, bf16[1,128,16,128]{3,2,1,0:T(8,128)(2,1)}, u32[]{:S(2)}) copy-start(bf16[1,128,16,128]{3,2,1,0:T(8,128)(2,1)} %param.8) | copy-start | bytes 1572868
  4.0 1.0 %copy-start.2 = (bf16[1,128,16,128]{3,2,1,0:T(8,128)(2,1)S(1)}, bf16[1,128,16,128]{3,2,1,0:T(8,128)(2,1)}, u32[]{:S(2)}) copy-start(bf16[1,128,16,128]{3,2,1,0:T(8,128)(2,1)} %param.9) | copy-start | bytes 1572868
  5.1 1.0 %copy-start.3 = (bf16[1,128,16,128]{3,2,1,0:T(8,128)(2,1)S(1)}, bf16[1,128,16,128]{3,2,1,0:T(8,128)(2,1)}, u32[]{:S(2)}) copy-start(bf16[1,128,16,128]{3,2,1,0:T(8,128)(2,1)} %param.6) | copy-start | bytes 1572868

commit v2 on v1

--- a/solution.py
+++ b/solution.py
@@ -12,6 +12,7 @@
 MESH = pl.DeviceIdType.MESH
 K, V, G, Q = 0, 1, 2, 3
 ZN = 16
+REACH = ZN // 4
 
 
 def iota(shape, dim):
@@ -34,6 +35,53 @@
     u = 1.0 + y
     d = u - 1.0
     return jnp.where(d == 0.0, y, jnp.log(u) * (y / jnp.where(d == 0.0, 1.0, d)))
+
+
+class Along:
+    def __init__(self, me, where, own, slots, ssem, rsem):
+        self.me, self.where = me, where
+        self.own, self.slots, self.ssem, self.rsem = own, slots, ssem, rsem
+
+    def copy(self, src, j, step):
+        return pltpu.make_async_remote_copy(
+            src_ref=self.own.at[src],
+            dst_ref=self.slots.at[j],
+            send_sem=self.ssem.at[j],
+            recv_sem=self.rsem.at[j],
+            device_id=self.where(lax.rem(self.me + step + ZN, ZN)),
+            device_id_type=MESH,
+        )
+
+    def near(self, j):
+        return self.copy(0, j, jnp.where(j < REACH, j + 1, REACH - 1 - j))
+
+    def start(self, row):
+        self.own[0] = row
+
+        def go(j, _):
+            self.near(j).start()
+            return 0
+
+        lax.fori_loop(0, 2 * REACH, go, 0)
+
+    def turn(self):
+        def go(j, _):
+            self.near(j).wait()
+            return 0
+
+        lax.fori_loop(0, 2 * REACH, go, 0)
+        below = jnp.sum(self.slots[0:REACH], axis=0)
+        above = jnp.sum(self.slots[REACH : 2 * REACH - 1], axis=0)
+        self.own[1] = below
+        self.own[2] = above
+        self.far = [self.copy(1, 2 * REACH, REACH), self.copy(2, 2 * REACH + 1, -REACH)]
+        for far in self.far:
+            far.start()
+
+    def finish(self):
+        for far in self.far:
+            far.wait()
+        return self.own[0] + jnp.sum(self.slots[...], axis=0)
 
 
 class Exchange:
@@ -71,11 +119,11 @@
 
 
 def kernel(
-    k_in, v_in, g_in, q_in, gw_ref, hb_ref,
+    k_in, v_in, g_in, q_in, gw_in, hb_in,
     qo_out, ko_out, gg_ref,
-    raw, raw32, sb, rb, colb, rowb, lastb, kvr, wts, qf, out_s, out_r, packed, lrow, square,
+    gw_v, hb_v, raw, raw32, sb, rb, colb, rowb, lastb, kvr, wts, qf, qgt, out_s, out_r, packed, lrow, square,
     wy_own, wy_slots, wz_own, wz_slots, dz_own, dz_slots, dy_own, dy_slots, dc_own, dc_slots,
-    lsem, osem, in_s, in_rs, back_s, back_rs, own_sem, own_back,
+    ssem, lsem, osem, in_s, in_rs, back_s, back_rs, own_sem, own_back,
     wy_s, wy_r, wz_s, wz_r, dz_s, dz_r, dy_s, dy_r, dc_s, dc_r,
 ):
     yn = wy_slots.shape[0]
@@ -101,11 +149,24 @@
         pltpu.make_async_copy(src, raw.at[a], lsem.at[a])
         for a, src in enumerate((k_in, v_in, g_in, q_in))
     ]
-    for load in loads:
+    small = [
+        pltpu.make_async_copy(src, dst, ssem.at[a])
+        for a, (src, dst) in enumerate(((gw_in, gw_v), (hb_in, hb_v)))
+    ]
+    for load in small + loads:
         load.start()
 
     barrier = pltpu.get_barrier_semaphore()
-    for n, me, where in ((ZN, z, at_z), (yn, yh, at_y), (heads, c, at_ctx)):
+
+    def greet_z(j, _):
+        step = jnp.where(j < REACH, j + 1, REACH - 1 - j)
+        pl.semaphore_signal(
+            barrier, inc=1, device_id=at_z(lax.rem(z + step + ZN, ZN)), device_id_type=MESH
+        )
+        return 0
+
+    lax.fori_loop(0, 2 * REACH, greet_z, 0)
+    for n, me, where in ((yn, yh, at_y), (heads, c, at_ctx)):
 
         def greet(j, _, n=n, me=me, where=where):
             pl.semaphore_signal(
@@ -115,13 +176,15 @@
 
         lax.fori_loop(1, n, greet, 0)
 
-    gw = gw_ref[...].astype(F32)
-    picked = jnp.sum(jnp.where(iota(gw.shape, 0) == c, gw, 0.0), axis=0, keepdims=True)
+    for load in small:
+        load.wait()
+    gw = gw_v[...].astype(F32)
+    picked = jnp.sum(jnp.where(iota(gw.shape, 1) == c, gw, 0.0), axis=1, keepdims=True)
     lane = iota((1, width), 1)
-    own_row = jnp.where(lane == 2 * i, picked[:, 0:1], 0.0) + jnp.where(
-        lane == 2 * i + 1, picked[:, 1:2], 0.0
+    own_row = jnp.where(lane == 2 * i, picked[0:1], 0.0) + jnp.where(
+        lane == 2 * i + 1, picked[1:2], 0.0
     )
-    hb = hb_ref[...].astype(F32)
+    hb = hb_v[...].astype(F32)
     bias = jnp.sum(jnp.where(iota(hb.shape, 1) == c, hb, 0.0), axis=1, keepdims=True)
 
     def split_heads(a):
@@ -161,9 +224,9 @@
         own_in(a).wait()
 
     wy = Exchange(yn, yh, at_y, wy_own, wy_slots, wy_s, wy_r)
-    wz = Exchange(ZN, z, at_z, wz_own, wz_slots, wz_s, wz_r)
+    wz = Along(z, at_z, wz_own, wz_slots, wz_s, wz_r)
     split_heads(K)
-    pl.semaphore_wait(barrier, (ZN - 1) + (yn - 1) + (heads - 1))
+    pl.semaphore_wait(barrier, 2 * REACH + (yn - 1) + (heads - 1))
     wy.start(own_row)
     send_heads(K)
     split_heads(V)
@@ -174,8 +237,8 @@
     send_heads(G)
     split_heads(Q)
     send_heads(Q)
-    wz.finish()
-    gate = jnp.sum(wz_slots[...], axis=0)
+    wz.turn()
+    gate = wz.finish()
 
     wait_heads(K)
     gate8 = jnp.broadcast_to(gate, (8, width)).astype(BF16)
@@ -243,24 +306,37 @@
 
     lax.fori_loop(1, heads, query_step, 0, unroll=3)
 
-    wait_heads(Q)
+    zeros = jnp.zeros((width, width), F32)
+
+    def arrival(b, dg_t):
+        gx, qx = rb[G, b], rb[Q, b]
+        qx32 = qx.astype(F32)
+        diff = jnp.sum(qx32 * qf[b], axis=1, keepdims=True)
+        qf[b] = dot(wts[b], qx, TN)
+        qgt[b] = dot(gx, (qx32 * jnp.exp(colb[b])).astype(BF16), TN)
+        return jnp.where(iota(dg_t.shape, 1) == b, diff, dg_t)
+
+    own_in(Q).wait()
+
+    def arrival_step(j, dg_t):
+        s = lax.rem(c + heads - j, heads)
+        bulk(Q, j, s, s).wait_recv()
+        return arrival(s, dg_t)
+
+    dg_t = lax.fori_loop(1, heads, arrival_step, arrival(c, zeros), unroll=3)
 
     def backward(j, carry):
         b = heads - 1 - j
         state, dg_t = carry
-        kx, vx, gx, qx = rb[K, b], rb[V, b], rb[G, b], rb[Q, b]
-        col, last = colb[b], lastb[b]
-        tail = jnp.exp(last - col)
-        kattn = dot(wts[b], qx, TN) + scale * tail * dot(vx, state.astype(BF16), NN)
+        last = lastb[b]
+        tail = jnp.exp(last - colb[b])
+        kattn = qf[b] + scale * tail * dot(rb[V, b], state.astype(BF16), NN)
         out_s[1, b] = kattn.astype(BF16)
-        qx32 = qx.astype(F32)
-        diff = jnp.sum(qx32 * qf[b] - kx.astype(F32) * kattn, axis=1, keepdims=True)
-        dg_t = jnp.where(iota(dg_t.shape, 1) == b, diff, dg_t)
-        scaled = (qx32 * jnp.exp(col)).astype(BF16)
-        return jnp.exp(last) * state + dot(gx, scaled, TN), dg_t
-
-    zeros = jnp.zeros((width, width), F32)
-    _, dg_t = lax.fori_loop(0, heads, backward, (zeros, zeros), unroll=4)
+        diff = jnp.sum(rb[K, b].astype(F32) * kattn, axis=1, keepdims=True)
+        dg_t = dg_t - jnp.where(iota(dg_t.shape, 1) == b, diff, 0.0)
+        return jnp.exp(last) * state + qgt[b], dg_t
+
+    _, dg_t = lax.fori_loop(0, heads, backward, (zeros, dg_t), unroll=4)
 
     later = (iota((tok, tok), 0) <= iota((tok, tok), 1)).astype(F32)
     within = dot(later, dg_t, NN, EXACT)
@@ -274,7 +350,7 @@
         total = total + dcol * rb[K, b].astype(F32)
         out_s[1, b] = (out_s[1, b].astype(F32) + dcol * gate).astype(BF16)
 
-    dz = Exchange(ZN, z, at_z, dz_own, dz_slots, dz_s, dz_r)
+    dz = Along(z, at_z, dz_own, dz_slots, dz_s, dz_r)
     dy = Exchange(yn, yh, at_y, dy_own, dy_slots, dy_s, dy_r)
     dc = Exchange(heads, c, at_ctx, dc_own, dc_slots, dc_s, dc_r)
     dz.start(jnp.sum(total, axis=0, keepdims=True))
@@ -302,17 +378,20 @@
         pltpu.make_async_copy(packed.at[which], outs[which], osem.at[which]).start()
 
     join_heads(0)
-    dz.finish()
-    dy.start(jnp.sum(dz_slots[...], axis=0))
+    dz.turn()
+    dy.start(dz.finish())
     dy.finish()
     dc.start(jnp.sum(dy_slots[...], axis=0))
     join_heads(1)
     dc.finish()
-    rows = dc_slots[...].reshape(heads, width)
-    at = iota((heads, width), 1)
-    left = jnp.sum(jnp.where(at == 2 * i, rows, 0.0), axis=1, keepdims=True)
-    right = jnp.sum(jnp.where(at == 2 * i + 1, rows, 0.0), axis=1, keepdims=True)
-    gg_ref[...] = jnp.where(iota((heads, 2), 1) == 0, left, right)
+    square[...] = jnp.zeros_like(square)
+    square[0:heads, :] = dc_slots[...].reshape(heads, width)
+    columns = square[...].T[:, 0:heads]
+    at = iota((width, heads), 0)
+    for e in range(2):
+        gg_ref[e : e + 1, :] = jnp.sum(
+            jnp.where(at == 2 * i + e, columns, 0.0), axis=0, keepdims=True
+        )
 
     def drain(j, _):
         t = lax.rem(c + j, heads)
@@ -327,6 +406,15 @@
         pltpu.make_async_copy(packed.at[which], outs[which], osem.at[which]).wait()
 
 
+def deliver(*refs):
+    *pairs, sem = refs
+    copies = [pltpu.make_async_copy(pairs[a], pairs[a + 3], sem.at[a]) for a in range(3)]
+    for copy in copies:
+        copy.start()
+    for copy in copies:
+        copy.wait()
+
+
 def per_device(queries, keys, values, out_grad, gate_weight, head_bias):
     _, tok, heads, width = queries.shape
     yn = lax.axis_size("dp") // ZN
@@ -338,19 +426,28 @@
     def slots(n):
         return [vm((1, width), F32), vm((n, 1, width), F32)]
 
+    along = [vm((3, 1, width), F32), vm((2 * REACH + 2, 1, width), F32)]
+    ends = dma((2 * REACH + 2,))
     anywhere = pl.BlockSpec(memory_space=pl.ANY)
+    far = pl.BlockSpec(memory_space=pltpu.HBM)
     inside = pl.BlockSpec(memory_space=pltpu.VMEM)
+    held = [
+        pltpu.with_memory_space_constraint(x, pltpu.HBM)
+        for x in (*flat, gate_weight.T, head_bias.reshape(1, heads))
+    ]
     qo, ko, gg = pl.pallas_call(
         kernel,
         name="history_grads",
         out_shape=(
             jax.ShapeDtypeStruct((rows, width), BF16),
             jax.ShapeDtypeStruct((rows, width), BF16),
-            jax.ShapeDtypeStruct((heads, 2), F32),
+            jax.ShapeDtypeStruct((2, heads), F32),
         ),
-        in_specs=[anywhere] * 4 + [inside] * 2,
+        in_specs=[far] * 6,
         out_specs=(anywhere, anywhere, inside),
         scratch_shapes=[
+            vm((2, heads), BF16),
+            vm((1, heads), BF16),
             vm((4, rows, width), BF16),
             vm((rows, width), F32),
             vm((4, heads, tok, width), BF16),
@@ -361,25 +458,35 @@
             vm((heads, width, width), BF16),
             vm((heads, tok, tok), BF16),
             vm((heads, tok, width), F32),
+            vm((heads, width, width), F32),
             vm((2, heads, tok, width), BF16),
             vm((2, heads, tok, width), BF16),
             vm((2, rows, width), BF16),
             vm((heads, width), F32),
             vm((width, width), F32),
-            *slots(yn), *slots(ZN), *slots(ZN), *slots(yn), *slots(heads),
-            dma((4,)), dma((2,)),
+            *slots(yn), *along, *along, *slots(yn), *slots(heads),
+            dma((2,)), dma((4,)), dma((2,)),
             dma((4, heads)), dma((4, heads)),
             dma((2, heads)), dma((2, heads)),
             dma((4,)), dma((2,)),
-            dma((yn,)), dma((yn,)), dma((ZN,)), dma((ZN,)),
-            dma((ZN,)), dma((ZN,)), dma((yn,)), dma((yn,)), dma((heads,)), dma((heads,)),
+            dma((yn,)), dma((yn,)), ends, ends,
+            ends, ends, dma((yn,)), dma((yn,)), dma((heads,)), dma((heads,)),
         ],
         compiler_params=pltpu.CompilerParams(
             collective_id=0, has_side_effects=True, vmem_limit_bytes=48 * 1024 * 1024
         ),
-    )(*flat, gate_weight, head_bias.reshape(1, heads))
+    )(*held)
+    outs = pl.pallas_call(
+        deliver,
+        name="deliver",
+        out_shape=tuple(jax.ShapeDtypeStruct(x.shape, x.dtype) for x in (qo, ko, gg)),
+        in_specs=[anywhere] * 3,
+        out_specs=(far,) * 3,
+        scratch_shapes=[dma((3,))],
+        compiler_params=pltpu.CompilerParams(vmem_limit_bytes=1024 * 1024),
+    )(qo, ko, gg)
     shape = (1, tok, heads, width)
-    return qo.reshape(shape), ko.reshape(shape), gg
+    return outs[0].reshape(shape), outs[1].reshape(shape), outs[2].T
 
 
 def solution(mesh):

time: 80.9 us -> 73.5 us (0.909)
  local copies, waits for them, and re-layouts: 7.69 us -> 0 us
    unnamed x16 -> x0, local copies, waits for them, and re-layouts: 7.69 us -> none
    pallas_call x0 -> x1, Pallas kernels: none -> 1 us  [per_device(): pl.pallas_call(deliver, name='deliver', out_shape=tuple((jax.ShapeDtypeSt...]
where the time goes in v2:
time: 73.5 us; the launch traced here: 73.3 us
  Pallas kernels  72.6 us (99%)
    pallas_call x1, Pallas kernels, per_device(): pl.pallas_call(kernel, name='history_grads', out_shape=(jax.ShapeDtypeStr...  71.7 us

profile of v2, /device:TPU:1, one launch (start us, length us, event | category | flops | bytes accessed | tf_op | source)
XLA Modules:
  0.0 73.3 jit_solution(18194780193328041335)
XLA Ops:
  0.6 71.7 %history_grads.1 = (bf16[2048,128]{1,0:T(8,128)(2,1)S(1)}, bf16[2048,128]{1,0:T(8,128)(2,1)S(1)}, f32[2,16]{1,0:T(2,128)S(1)}) custom-call(bf16[2048,128]{1,0:T(8,128)(2,1)} %bitcast.9, bf16[2048,128]{1,0:T(8,128)(2,1)} %bitcast.10, bf16[2048,128]{1,0:T(8,128)(2,1)} %bitcast.11, bf16[2048,128]{1,0:T(8,128)(2,1)} %bitcast.12, bf16[2,16]{1,0:T(2,128)(2,1)} %bitcast.13, ...), custom_call_target="tpu_custom_call" | custom-call | tf_op jit(solution)/shard_map/history_grads/pallas_call | solution.py:438
  72.3 1.0 %deliver.1 = (bf16[2048,128]{1,0:T(8,128)(2,1)}, bf16[2048,128]{1,0:T(8,128)(2,1)}, f32[2,16]{1,0:T(2,128)}) custom-call(bf16[2048,128]{1,0:T(8,128)(2,1)S(1)} %get-tuple-element.9.refs_0_, bf16[2048,128]{1,0:T(8,128)(2,1)S(1)} %get-tuple-element.10.refs_1_, f32[2,16]{1,0:T(2,128)S(1)} %get-tuple-element.11.refs_2_), custom_call_target="tpu_custom_call" | custom-call | tf_op jit(solution)/shard_map/deliver/pallas_call | solution.py:479

commit v3 on v2

--- a/solution.py
+++ b/solution.py
@@ -89,42 +89,41 @@
         self.n, self.me, self.where = n, me, where
         self.own, self.slots, self.ssem, self.rsem = own, slots, ssem, rsem
 
-    def copy(self, j, slot, target):
-        return pltpu.make_async_remote_copy(
-            src_ref=self.own,
-            dst_ref=self.slots.at[slot],
-            send_sem=self.ssem.at[j],
-            recv_sem=self.rsem.at[slot],
-            device_id=self.where(target),
-            device_id_type=MESH,
-        )
-
     def start(self, row):
         self.own[...] = row
         self.slots[self.me] = row
 
         def go(j, _):
-            self.copy(j, self.me, lax.rem(self.me + j, self.n)).start()
-            return 0
-
-        lax.fori_loop(1, self.n, go, 0)
+            pltpu.make_async_remote_copy(
+                src_ref=self.own,
+                dst_ref=self.slots.at[self.me],
+                send_sem=self.ssem,
+                recv_sem=self.rsem,
+                device_id=self.where(lax.rem(self.me + j, self.n)),
+                device_id_type=MESH,
+            ).start()
+            return 0
+
+        lax.fori_loop(1, self.n, go, 0, unroll=3)
+
+    def wait(self, sem):
+        rows = self.slots.at[pl.ds(0, self.n - 1)]
+        pltpu.make_async_copy(rows, rows, sem).wait()
 
     def finish(self):
-        def go(j, _):
-            s = lax.rem(self.me + j, self.n)
-            self.copy(j, s, s).wait()
-            return 0
-
-        lax.fori_loop(1, self.n, go, 0)
+        self.wait(self.rsem)
+
+    def drain(self):
+        self.wait(self.ssem)
 
 
 def kernel(
     k_in, v_in, g_in, q_in, gw_in, hb_in,
     qo_out, ko_out, gg_ref,
     gw_v, hb_v, raw, raw32, sb, rb, colb, rowb, lastb, kvr, wts, qf, qgt, out_s, out_r, packed, lrow, square,
-    wy_own, wy_slots, wz_own, wz_slots, dz_own, dz_slots, dy_own, dy_slots, dc_own, dc_slots,
+    wy_own, wy_slots, wz_own, wz_slots, dz_own, dz_slots, dc_own, dc_slots,
     ssem, lsem, osem, in_s, in_rs, back_s, back_rs, own_sem, own_back,
-    wy_s, wy_r, wz_s, wz_r, dz_s, dz_r, dy_s, dy_r, dc_s, dc_r,
+    wy_s, wy_r, wz_s, wz_r, dz_s, dz_r, dc_s, dc_r,
 ):
     yn = wy_slots.shape[0]
     heads = sb.shape[1]
@@ -295,16 +294,11 @@
         qf[b] = full
         out_s[0, b] = full.astype(BF16)
 
-    query_block(c)
-    own_out(0).start()
-
     def query_step(j, _):
-        b = lax.rem(c + j, heads)
-        query_block(b)
-        back(0, j, c, b).start()
+        query_block(j)
         return 0
 
-    lax.fori_loop(1, heads, query_step, 0, unroll=3)
+    lax.fori_loop(0, heads, query_step, 0, unroll=4)
 
     zeros = jnp.zeros((width, width), F32)
 
@@ -324,6 +318,16 @@
         return arrival(s, dg_t)
 
     dg_t = lax.fori_loop(1, heads, arrival_step, arrival(c, zeros), unroll=3)
+
+    def send_back(which):
+        def go(j, _):
+            back(which, j, c, lax.rem(c + j, heads)).start()
+            return 0
+
+        lax.fori_loop(1, heads, go, 0)
+        own_out(which).start()
+
+    send_back(0)
 
     def backward(j, carry):
         b = heads - 1 - j
@@ -350,18 +354,14 @@
         total = total + dcol * rb[K, b].astype(F32)
         out_s[1, b] = (out_s[1, b].astype(F32) + dcol * gate).astype(BF16)
 
-    dz = Along(z, at_z, dz_own, dz_slots, dz_s, dz_r)
-    dy = Exchange(yn, yh, at_y, dy_own, dy_slots, dy_s, dy_r)
-    dc = Exchange(heads, c, at_ctx, dc_own, dc_slots, dc_s, dc_r)
+    dz = Exchange(ZN, z, at_z, dz_own, dz_slots, dz_s, dz_r)
+    def at_cell(t):
+        return {"dp": t // heads * ZN + z, "ctx": lax.rem(t, heads)}
+
+    dc = Exchange(yn * heads, yh * heads + c, at_cell, dc_own, dc_slots, dc_s, dc_r)
     dz.start(jnp.sum(total, axis=0, keepdims=True))
 
-    def send_key(j, _):
-        back(1, j, c, lax.rem(c + j, heads)).start()
-        return 0
-
-    lax.fori_loop(1, heads, send_key, 0)
-    own_out(1).start()
-
+    send_back(1)
     outs = (qo_out, ko_out)
 
     def join_heads(which):
@@ -378,20 +378,22 @@
         pltpu.make_async_copy(packed.at[which], outs[which], osem.at[which]).start()
 
     join_heads(0)
-    dz.turn()
-    dy.start(dz.finish())
-    dy.finish()
-    dc.start(jnp.sum(dy_slots[...], axis=0))
+    dz.finish()
+    dc.start(jnp.sum(dz_slots[...], axis=0))
     join_heads(1)
     dc.finish()
+    rows = jnp.sum(dc_slots[...].reshape(yn, heads, width), axis=0)
     square[...] = jnp.zeros_like(square)
-    square[0:heads, :] = dc_slots[...].reshape(heads, width)
+    square[0:heads, :] = rows
     columns = square[...].T[:, 0:heads]
     at = iota((width, heads), 0)
     for e in range(2):
         gg_ref[e : e + 1, :] = jnp.sum(
             jnp.where(at == 2 * i + e, columns, 0.0), axis=0, keepdims=True
         )
+
+    for small_exchange in (wy, dz, dc):
+        small_exchange.drain()
 
     def drain(j, _):
         t = lax.rem(c + j, heads)
@@ -428,6 +430,7 @@
 
     along = [vm((3, 1, width), F32), vm((2 * REACH + 2, 1, width), F32)]
     ends = dma((2 * REACH + 2,))
+    one = dma(())
     anywhere = pl.BlockSpec(memory_space=pl.ANY)
     far = pl.BlockSpec(memory_space=pltpu.HBM)
     inside = pl.BlockSpec(memory_space=pltpu.VMEM)
@@ -464,13 +467,12 @@
             vm((2, rows, width), BF16),
             vm((heads, width), F32),
             vm((width, width), F32),
-            *slots(yn), *along, *along, *slots(yn), *slots(heads),
+            *slots(yn), *along, *slots(ZN), *slots(yn * heads),
             dma((2,)), dma((4,)), dma((2,)),
             dma((4, heads)), dma((4, heads)),
             dma((2, heads)), dma((2, heads)),
             dma((4,)), dma((2,)),
-            dma((yn,)), dma((yn,)), ends, ends,
-            ends, ends, dma((yn,)), dma((yn,)), dma((heads,)), dma((heads,)),
+            one, one, ends, ends, one, one, one, one,
         ],
         compiler_params=pltpu.CompilerParams(
             collective_id=0, has_side_effects=True, vmem_limit_bytes=48 * 1024 * 1024

time: 73.5 us -> 68.4 us (0.931)
  Pallas kernels: 72.6 us -> 67.6 us
    pallas_call x1, Pallas kernels: 71.7 us -> 66.6 us  [per_device(): pl.pallas_call(kernel, name='history_grads', out_shape=(jax.ShapeDtypeStr...]
where the time goes in v3:
time: 68.4 us; the launch traced here: 68.2 us
  Pallas kernels  67.6 us (99%)
    pallas_call x1, Pallas kernels, per_device(): pl.pallas_call(kernel, name='history_grads', out_shape=(jax.ShapeDtypeStr...  66.6 us

profile of v3, /device:TPU:1, one launch (start us, length us, event | category | flops | bytes accessed | tf_op | source)
XLA Modules:
  0.0 68.2 jit_solution(1291237919776860971)
XLA Ops:
  0.6 66.6 %history_grads.1 = (bf16[2048,128]{1,0:T(8,128)(2,1)S(1)}, bf16[2048,128]{1,0:T(8,128)(2,1)S(1)}, f32[2,16]{1,0:T(2,128)S(1)}) custom-call(bf16[2048,128]{1,0:T(8,128)(2,1)} %bitcast.9, bf16[2048,128]{1,0:T(8,128)(2,1)} %bitcast.10, bf16[2048,128]{1,0:T(8,128)(2,1)} %bitcast.11, bf16[2048,128]{1,0:T(8,128)(2,1)} %bitcast.12, bf16[2,16]{1,0:T(2,128)(2,1)} %bitcast.13, ...), custom_call_target="tpu_custom_call" | custom-call | tf_op jit(solution)/shard_map/history_grads/pallas_call | solution.py:441
  67.2 1.0 %deliver.1 = (bf16[2048,128]{1,0:T(8,128)(2,1)}, bf16[2048,128]{1,0:T(8,128)(2,1)}, f32[2,16]{1,0:T(2,128)}) custom-call(bf16[2048,128]{1,0:T(8,128)(2,1)S(1)} %get-tuple-element.9.refs_0_, bf16[2048,128]{1,0:T(8,128)(2,1)S(1)} %get-tuple-element.10.refs_1_, f32[2,16]{1,0:T(2,128)S(1)} %get-tuple-element.11.refs_2_), custom_call_target="tpu_custom_call" | custom-call | tf_op jit(solution)/shard_map/deliver/pallas_call | solution.py:481

commit v4 on v3

--- a/solution.py
+++ b/solution.py
@@ -11,6 +11,7 @@
 BF16 = jnp.bfloat16
 MESH = pl.DeviceIdType.MESH
 K, V, G, Q = 0, 1, 2, 3
+PIECES = 4
 ZN = 16
 REACH = ZN // 4
 
@@ -229,14 +230,14 @@
     wy.start(own_row)
     send_heads(K)
     split_heads(V)
-    send_heads(V)
+    split_heads(G)
+    split_heads(Q)
     wy.finish()
     wz.start(jnp.sum(wy_slots[...], axis=0))
-    split_heads(G)
+    send_heads(V)
+    wz.turn()
     send_heads(G)
-    split_heads(Q)
     send_heads(Q)
-    wz.turn()
     gate = wz.finish()
 
     wait_heads(K)
@@ -300,6 +301,16 @@
 
     lax.fori_loop(0, heads, query_step, 0, unroll=4)
 
+    def send_back(which):
+        def go(j, _):
+            back(which, j, c, lax.rem(c + j, heads)).start()
+            return 0
+
+        lax.fori_loop(1, heads, go, 0)
+        own_out(which).start()
+
+    send_back(0)
+
     zeros = jnp.zeros((width, width), F32)
 
     def arrival(b, dg_t):
@@ -318,16 +329,6 @@
         return arrival(s, dg_t)
 
     dg_t = lax.fori_loop(1, heads, arrival_step, arrival(c, zeros), unroll=3)
-
-    def send_back(which):
-        def go(j, _):
-            back(which, j, c, lax.rem(c + j, heads)).start()
-            return 0
-
-        lax.fori_loop(1, heads, go, 0)
-        own_out(which).start()
-
-    send_back(0)
 
     def backward(j, carry):
         b = heads - 1 - j
@@ -352,15 +353,13 @@
     for b in range(heads):
         dcol = jnp.broadcast_to(dlogit[:, b : b + 1], (tok, width))
         total = total + dcol * rb[K, b].astype(F32)
+
+    dz = Exchange(ZN, z, at_z, dz_own, dz_slots, dz_s, dz_r)
+    dz.start(jnp.sum(total, axis=0, keepdims=True))
+
+    for b in range(heads):
+        dcol = jnp.broadcast_to(dlogit[:, b : b + 1], (tok, width))
         out_s[1, b] = (out_s[1, b].astype(F32) + dcol * gate).astype(BF16)
-
-    dz = Exchange(ZN, z, at_z, dz_own, dz_slots, dz_s, dz_r)
-    def at_cell(t):
-        return {"dp": t // heads * ZN + z, "ctx": lax.rem(t, heads)}
-
-    dc = Exchange(yn * heads, yh * heads + c, at_cell, dc_own, dc_slots, dc_s, dc_r)
-    dz.start(jnp.sum(total, axis=0, keepdims=True))
-
     send_back(1)
     outs = (qo_out, ko_out)
 
@@ -379,9 +378,47 @@
 
     join_heads(0)
     dz.finish()
-    dc.start(jnp.sum(dz_slots[...], axis=0))
+    row = jnp.sum(dz_slots[...], axis=0)
+    dc_own[...] = row
+    mine = yh * heads + c
+    dc_slots[mine] = row
+
+    def to_cell(y, t):
+        pltpu.make_async_remote_copy(
+            src_ref=dc_own,
+            dst_ref=dc_slots.at[mine],
+            send_sem=dc_s,
+            recv_sem=dc_r,
+            device_id={"dp": y * ZN + z, "ctx": t},
+            device_id_type=MESH,
+        ).start()
+        return 0
+
+    for step in (2, 1, 3):
+        y = lax.rem(yh + step, yn)
+        lax.fori_loop(0, heads, lambda t, _, y=y: to_cell(y, t), 0, unroll=8)
+    lax.fori_loop(1, heads, lambda j, _: to_cell(yh, lax.rem(c + j, heads)), 0, unroll=5)
+
+    def wait_cells(sem):
+        others = dc_slots.at[pl.ds(0, yn * heads - 1)]
+        pltpu.make_async_copy(others, others, sem).wait()
+
     join_heads(1)
-    dc.finish()
+    for exchange in (wy, dz):
+        exchange.drain()
+
+    def drain(j, _):
+        t = lax.rem(c + j, heads)
+        for a in range(4):
+            bulk(a, j, c, t).wait_send()
+        for which in range(2):
+            back(which, j, c, t).wait_send()
+        return 0
+
+    lax.fori_loop(1, heads, drain, 0)
+    for which in range(2):
+        pltpu.make_async_copy(packed.at[which], outs[which], osem.at[which]).wait()
+    wait_cells(dc_r)
     rows = jnp.sum(dc_slots[...].reshape(yn, heads, width), axis=0)
     square[...] = jnp.zeros_like(square)
     square[0:heads, :] = rows
@@ -392,25 +429,17 @@
             jnp.where(at == 2 * i + e, columns, 0.0), axis=0, keepdims=True
         )
 
-    for small_exchange in (wy, dz, dc):
-        small_exchange.drain()
-
-    def drain(j, _):
-        t = lax.rem(c + j, heads)
-        for a in range(4):
-            bulk(a, j, c, t).wait_send()
-        for which in range(2):
-            back(which, j, c, t).wait_send()
-        return 0
-
-    lax.fori_loop(1, heads, drain, 0)
-    for which in range(2):
-        pltpu.make_async_copy(packed.at[which], outs[which], osem.at[which]).wait()
-
-
-def deliver(*refs):
-    *pairs, sem = refs
-    copies = [pltpu.make_async_copy(pairs[a], pairs[a + 3], sem.at[a]) for a in range(3)]
+    wait_cells(dc_s)
+
+
+def deliver(qo, ko, gg, qo_out, ko_out, gg_out, sem):
+    rows = qo.shape[0] // PIECES
+    copies = [pltpu.make_async_copy(gg, gg_out, sem.at[2 * PIECES])]
+    for piece in range(PIECES):
+        part = pl.ds(piece * rows, rows)
+        for which, (src, dst) in enumerate(((qo, qo_out), (ko, ko_out))):
+            at = sem.at[2 * piece + which]
+            copies.append(pltpu.make_async_copy(src.at[part], dst.at[part], at))
     for copy in copies:
         copy.start()
     for copy in copies:
@@ -484,7 +513,7 @@
         out_shape=tuple(jax.ShapeDtypeStruct(x.shape, x.dtype) for x in (qo, ko, gg)),
         in_specs=[anywhere] * 3,
         out_specs=(far,) * 3,
-        scratch_shapes=[dma((3,))],
+        scratch_shapes=[dma((2 * PIECES + 1,))],
         compiler_params=pltpu.CompilerParams(vmem_limit_bytes=1024 * 1024),
     )(qo, ko, gg)
     shape = (1, tok, heads, width)

time: 68.4 us -> 65.9 us (0.963)
  Pallas kernels: 67.6 us -> 65.1 us
    pallas_call x1, Pallas kernels: 66.6 us -> 64.1 us  [per_device(): pl.pallas_call(kernel, name='history_grads', out_shape=(jax.ShapeDtypeStr...]
where the time goes in v4:
time: 65.9 us; the launch traced here: 65.7 us
  Pallas kernels  65.1 us (99%)
    pallas_call x1, Pallas kernels, per_device(): pl.pallas_call(kernel, name='history_grads', out_shape=(jax.ShapeDtypeStr...  64.1 us

profile of v4, /device:TPU:1, one launch (start us, length us, event | category | flops | bytes accessed | tf_op | source)
XLA Modules:
  0.0 65.7 jit_solution(9221901406478764586)
XLA Ops:
  0.6 64.1 %history_grads.1 = (bf16[2048,128]{1,0:T(8,128)(2,1)S(1)}, bf16[2048,128]{1,0:T(8,128)(2,1)S(1)}, f32[2,16]{1,0:T(2,128)S(1)}) custom-call(bf16[2048,128]{1,0:T(8,128)(2,1)} %bitcast.9, bf16[2048,128]{1,0:T(8,128)(2,1)} %bitcast.10, bf16[2048,128]{1,0:T(8,128)(2,1)} %bitcast.11, bf16[2048,128]{1,0:T(8,128)(2,1)} %bitcast.12, bf16[2,16]{1,0:T(2,128)(2,1)} %bitcast.13, ...), custom_call_target="tpu_custom_call" | custom-call | tf_op jit(solution)/shard_map/history_grads/pallas_call | solution.py:470
  64.7 1.0 %deliver.1 = (bf16[2048,128]{1,0:T(8,128)(2,1)}, bf16[2048,128]{1,0:T(8,128)(2,1)}, f32[2,16]{1,0:T(2,128)}) custom-call(bf16[2048,128]{1,0:T(8,128)(2,1)S(1)} %get-tuple-element.9.qo, bf16[2048,128]{1,0:T(8,128)(2,1)S(1)} %get-tuple-element.10.ko, f32[2,16]{1,0:T(2,128)S(1)} %get-tuple-element.11.gg), custom_call_target="tpu_custom_call" | custom-call | tf_op jit(solution)/shard_map/deliver/pallas_call | solution.py:510
